TPU v7x, 32 devices: a whole 2x2x4 slice. The times are simulated.
32 devices in a mesh: seq: 8 (over z, x), tp: 4 (over y, core).
Axes of the slice: x: 2, y: 2, z: 4, core: 2. Of those that a mesh axis runs over, the one named last changes fastest.
Arguments:
- tokens_in: bfloat16 [4, 16, 1024], replicated, may hold values from -6 to 6
- key_cache: bfloat16 [16, 2048, 1024], P(None, 'seq', 'tp'), may hold values from -6 to 6
- value_cache: bfloat16 [16, 2048, 1024], P(None, 'seq', 'tp'), may hold values from -6 to 6
- cache_len: int32 [16], replicated, may hold values from 1 to 2048, as said below
- bucket_table: int32 [2052], replicated, may hold values from 0 to 31, as said below
- rel_bias: float32 [32, 16], P(None, 'tp'), may hold values from -4 to 283
- attn_gain: float32 [1024], replicated, may hold values from 0.1 to 1.9
- moe_gain: float32 [1024], replicated, may hold values from 0.1 to 1.9
- w_qkv: bfloat16 [3, 1024, 1024], P(None, None, 'tp'), may hold values from -0.1875 to 0.1875
- w_out: bfloat16 [1024, 1024], P('tp'), may hold values from -0.1875 to 0.1875
- router: bfloat16 [1024, 16], replicated, may hold values from -0.1875 to 0.1875
- expert_choice: int32 [4, 16, 2], replicated, may hold values from 0 to 15, all different within a row
- w_gate_up: bfloat16 [2, 45056, 1024], P(None, ('seq', 'tp')), may hold values from -0.1875 to 0.1875
- w_down: bfloat16 [45056, 1024], P(('seq', 'tp')), may hold values from -0.109375 to 0.109375
Outputs:
- layer_out: bfloat16 [4, 16, 1024], replicated
Inputs may be any that keep to these rules, and one draw needn't show every extreme that they name: Request r's cache holds its positions 0 to cache_len[r] - 1; some request holds exactly 2048. `bucket_table`: non-decreasing in the distance, 0 at distance 0. `expert_choice`: the 2 experts of a token differ.
All inputs are finite; a program needn't handle non-finite values.
Results may differ from a plain program's by a relative error of at most 0.012.
Values sent between devices are 32-bit elements; how exact they have to be, the bound alone decides.
No kernel may reach another device: no remote copies, remote signals or barrier semaphores. Data moves between devices by JAX's collectives and lax.ppermute only.
A program may use at most 64 MiB of HBM per device.

v0:
```python
import jax
import jax.numpy as jnp
from jax import lax
from jax.sharding import PartitionSpec as P

HEAD_DIM = 64
FF = 2816
NEG = -1e30
EPS = 1e-06


def rms_scale(values, gain_vec):
    return values * lax.rsqrt(jnp.mean(values * values, axis=-1, keepdims=True) + EPS) * gain_vec


def on_device(
    tokens_in,
    key_cache,
    value_cache,
    cache_len,
    bucket_table,
    rel_bias,
    attn_gain,
    moe_gain,
    w_qkv,
    w_out,
    router,
    expert_choice,
    w_gate_up,
    w_down,
):
    steps_all, requests, model_width = tokens_in.shape
    cache_rows = key_cache.shape[1]
    heads_local = key_cache.shape[2] // HEAD_DIM
    table_len = bucket_table.shape[0]
    num_buckets = rel_bias.shape[0]
    num_experts = router.shape[1]
    hidden_local = w_down.shape[0]
    bucket_ids = jnp.arange(num_buckets, dtype=jnp.int32)

    def bias_lookup(buckets, pattern):
        onehot = (buckets[..., None] == bucket_ids).astype(jnp.float32)
        return jnp.einsum(pattern, onehot, rel_bias, precision=lax.Precision.HIGHEST)

    normed = rms_scale(tokens_in.astype(jnp.float32), attn_gain).astype(jnp.bfloat16)
    projected = jnp.einsum(
        "srd,kdf->ksrf", normed, w_qkv, preferred_element_type=jnp.float32
    ).astype(jnp.bfloat16)
    head_shape = (steps_all, requests, heads_local, HEAD_DIM)
    queries = projected[0].reshape(head_shape)
    fresh_keys = projected[1].reshape(head_shape)
    fresh_values = projected[2].reshape(head_shape)
    keys_heads = key_cache.reshape(requests, cache_rows, heads_local, HEAD_DIM)
    values_heads = value_cache.reshape(requests, cache_rows, heads_local, HEAD_DIM)
    positions = lax.axis_index("seq") * cache_rows + jnp.arange(cache_rows, dtype=jnp.int32)
    live_rows = positions[None, :] < cache_len[:, None]

    def cache_part(query_blk, step_ids, keys_blk, vals_blk, lens_blk, live_blk):
        scores = jnp.einsum(
            "srhd,rchd->srhc", query_blk, keys_blk, preferred_element_type=jnp.float32
        )
        distance = lens_blk[None, :, None] + step_ids[:, None, None] - positions[None, None, :]
        buckets = jnp.take(bucket_table, jnp.clip(distance, 0, table_len - 1))
        scores = scores + bias_lookup(buckets, "srcb,bh->srhc")
        usable = live_blk[None, :, None, :]
        scores = jnp.where(usable, scores, NEG)
        maxima = jnp.max(scores, axis=-1)
        weights = jnp.where(usable, jnp.exp(scores - maxima[..., None]), 0.0)
        summed = jnp.einsum(
            "srhc,rchd->srhd", weights, vals_blk, preferred_element_type=jnp.float32
        )
        return (maxima, jnp.sum(weights, axis=-1), summed)

    def attend_cache(query_blk, step_ids):
        return cache_part(query_blk, step_ids, keys_heads, values_heads, cache_len, live_rows)

    def merge_cache(maxima, totals, summed):
        overall = lax.pmax(maxima, "seq")
        factor = jnp.exp(maxima - overall)
        totals, summed = lax.psum((totals * factor, summed * factor[..., None]), "seq")
        return (overall, totals, summed)

    def attend_recent(query_blk, step_ids):
        scores = jnp.einsum(
            "srhd,jrhd->srhj", query_blk, fresh_keys, preferred_element_type=jnp.float32
        )
        distance = step_ids[:, None] - jnp.arange(steps_all, dtype=jnp.int32)[None, :]
        buckets = jnp.take(bucket_table, jnp.clip(distance, 0, table_len - 1))
        scores = scores + bias_lookup(buckets, "sjb,bh->shj")[:, None]
        usable = (distance >= 0)[:, None, None, :]
        scores = jnp.where(usable, scores, NEG)
        maxima = jnp.max(scores, axis=-1)
        weights = jnp.where(usable, jnp.exp(scores - maxima[..., None]), 0.0)
        summed = jnp.einsum(
            "srhj,jrhd->srhd", weights, fresh_values, preferred_element_type=jnp.float32
        )
        return (maxima, jnp.sum(weights, axis=-1), summed)

    first_col = (lax.axis_index("seq") * lax.axis_size("tp") + lax.axis_index("tp")) * hidden_local
    col_expert = (first_col + jnp.arange(hidden_local, dtype=jnp.int32)) // FF
    owner = (col_expert[None, :] == jnp.arange(num_experts, dtype=jnp.int32)[:, None]).astype(
        jnp.float32
    )

    def layer(start, step_count):
        step_ids = jnp.arange(start, start + step_count, dtype=jnp.int32)
        query_blk = queries[start : start + step_count]
        cache_max, cache_tot, cache_sum = merge_cache(*attend_cache(query_blk, step_ids))
        new_max, new_tot, new_sum = attend_recent(query_blk, step_ids)
        joint = jnp.maximum(cache_max, new_max)
        scale_cache = jnp.exp(cache_max - joint)
        scale_new = jnp.exp(new_max - joint)
        totals = cache_tot * scale_cache + new_tot * scale_new
        summed = cache_sum * scale_cache[..., None] + new_sum * scale_new[..., None]
        attended = (
            (summed / totals[..., None])
            .reshape(step_count, requests, heads_local * HEAD_DIM)
            .astype(jnp.bfloat16)
        )
        partial_value = jnp.einsum(
            "srf,fd->srd", attended, w_out, preferred_element_type=jnp.float32
        )
        mid = tokens_in[start : start + step_count].astype(jnp.float32) + lax.psum(
            partial_value, "tp"
        )
        moe_in = rms_scale(mid, moe_gain).astype(jnp.bfloat16)
        logits = jnp.einsum("srd,de->sre", moe_in, router, preferred_element_type=jnp.float32)
        picked = expert_choice[start : start + step_count][..., None] == jnp.arange(
            num_experts, dtype=jnp.int32
        )
        chosen = jnp.sum(jnp.where(picked, logits[:, :, None, :], 0.0), axis=-1)
        leading = jax.nn.sigmoid(chosen[..., 0] - chosen[..., 1])
        gate_pair = jnp.stack([leading, 1.0 - leading], axis=-1)
        per_expert = jnp.sum(jnp.where(picked, gate_pair[..., None], 0.0), axis=2)
        coef = jnp.einsum("sre,ef->srf", per_expert, owner, precision=lax.Precision.HIGHEST)
        gate_up = jnp.einsum("srd,kfd->ksrf", moe_in, w_gate_up, preferred_element_type=jnp.float32)
        hidden = (jax.nn.gelu(gate_up[0], approximate=True) * gate_up[1] * coef).astype(
            jnp.bfloat16
        )
        expert_part = jnp.einsum("srf,fd->srd", hidden, w_down, preferred_element_type=jnp.float32)
        mixture = lax.psum(expert_part, ("seq", "tp"))
        return (mid + mixture).astype(jnp.bfloat16)

    return layer(0, steps_all)


def solution(mesh):
    return jax.shard_map(
        on_device,
        mesh=mesh,
        in_specs=(
            P(),
            P(None, "seq", "tp"),
            P(None, "seq", "tp"),
            P(),
            P(),
            P(None, "tp"),
            P(),
            P(),
            P(None, None, "tp"),
            P("tp", None),
            P(),
            P(),
            P(None, ("seq", "tp"), None),
            P(("seq", "tp"), None),
        ),
        out_specs=P(),
        check_vma=False,
    )
```

profile of v0, /device:TPU:0, one launch (start us, length us, event | category | flops | bytes accessed | tf_op | source)
XLA Modules:
  0.0 400.7 jit_solution(13281460656458387013)
XLA Ops:
  6.5 0.8 iota_add_fusion.1
  7.4 0.8 broadcast_compare_fusion
  8.2 0.1 compare_select_fusion
  8.3 90.5 %gather_fusion = s32[16384]{0:T(1024)S(1)} fusion(s32[2052]{0:T(1024)S(1)} %copy-done.1, s32[16384]{0:T(1024)S(1)} %broadcast_clamp_fusion), kind=kCustom, calls=%fused_computation | custom fusion | bytes 196608 | tf_op jit(solution)/shard_map/jit(_take)/gather | solution.py:63
  98.9 0.1 fusion.59
  99.0 0.1 fusion.37
  99.2 1.8 fusion.23
  101.0 0.6 fusion.78
  101.6 0.1 reshape_squeeze.9
  101.7 4.0 copy.81
  105.7 0.7 fusion.8
  106.4 2.1 fusion.80
  108.6 38.8 %pmax.7 = f32[4,16,4]{0,2,1:T(4,128)S(1)} all-reduce(f32[4,16,4]{0,2,1:T(4,128)S(1)} %get-tuple-element.17), channel_id=1, replica_groups=mesh['seq'=8,'tp'=4] {'seq'}, use_global_device_ids=true, to_apply=%region_2.3 | all-reduce | flops 256 | bytes 2048 | tf_op jit(solution)/shard_map/pmax | solution.py:78
  147.4 0.3 fusion.40
  147.7 3.9 copy.84
  151.7 3.0 fusion.16
  154.6 0.0 all-reduce.4.cloned.1.call-update
  154.7 0.0 all-reduce.6.cloned.1.call-start
  154.7 33.7 %psum.29 = f32[4,16,4]{0,2,1:T(4,128)} all-reduce(f32[4,16,4]{0,2,1:T(4,128)S(1)} %bitcast.133), channel_id=1, replica_groups=mesh['seq'=8,'tp'=4] {'seq'}, use_global_device_ids=true, to_apply=%region_6.7 | all-reduce | flops 256 | bytes 2048 | tf_op jit(solution)/shard_map/psum | solution.py:80
  188.4 0.7 reshape_squeeze.10
  189.1 0.1 copy.85
  189.2 0.1 reshape.206
  189.3 0.7 gather_fusion.1
  190.0 0.1 reshape.205
  190.1 0.2 convolution_bitcast_fusion.4
  190.3 0.1 copy.88
  190.4 1.2 fusion.81
  191.6 0.6 copy-done.7
  192.3 0.1 fusion.51
  192.4 1.4 multiply_add_fusion
  193.9 1.5 reshape_squeeze.11
  195.3 26.5 %all-reduce.4.cloned.1.call-done = f32[4,16,4,64]{3,0,2,1:T(4,128)} async-done(((f32[4,16,4,64]{3,0,2,1:T(4,128)}), f32[4,16,4,64]{3,0,2,1:T(4,128)}) %all-reduce.4.cloned.1.call-update) | async-done | bytes 65552 | tf_op jit(solution)/shard_map/psum | solution.py:80
  221.9 1.4 fusion.22
  223.2 0.7 copy.91
  223.9 1.6 convert_element_type.36
  225.5 1.7 fusion.27
  227.1 0.0 all-reduce.8.cloned.1.call-start
  227.2 31.3 %all-reduce.6.cloned.1.call-done = f32[4,16,1024]{2,1,0:T(8,128)} async-done(((f32[4,16,1024]{2,1,0:T(8,128)}), f32[4,16,1024]{2,1,0:T(8,128)}) %all-reduce.6.cloned.1.call-update) | async-done | bytes 262160 | tf_op jit(solution)/shard_map/psum | solution.py:123
  258.5 1.1 multiply_reduce_fusion
  259.6 1.1 multiply_convert_fusion
  260.7 4.5 %fusion.4 = f32[2,4,16,1408]{3,2,0,1:T(8,128)S(1)} fusion(bf16[2,1408,1024]{2,1,0:T(8,128)(2,1)} %param.26, bf16[4,16,1024]{2,1,0:T(8,128)(2,1)S(1)} %multiply_convert_fusion), kind=kOutput, calls=%fused_computation.6 | convolution fusion | flops 369098752 | bytes 6619136 | tf_op jit(solution)/shard_map/srd,kfd->ksrf/dot_general | solution.py:136
  265.2 0.2 fusion.66
  265.4 0.2 select_reduce_fusion.1
  265.6 0.1 select_reduce_fusion
  265.7 0.3 fusion.7
  266.1 1.3 fusion.2
  267.5 125.1 %all-reduce.8.cloned.1.call-done = f32[4,16,1024]{2,1,0:T(8,128)} async-done(((f32[4,16,1024]{2,1,0:T(8,128)}), f32[4,16,1024]{2,1,0:T(8,128)}) %all-reduce.8.cloned.1.call-update) | async-done | bytes 262160 | tf_op jit(solution)/shard_map/psum | solution.py:141
  392.5 1.6 add_convert_fusion
  (46 shorter events, 0.3 us)
Async XLA Ops:
  6.5 259.5 %copy-start = (bf16[1408,1024]{1,0:T(8,128)(2,1)S(1)}, bf16[1408,1024]{1,0:T(8,128)(2,1)}, u32[]{:S(2)}) copy-start(bf16[1408,1024]{1,0:T(8,128)(2,1)} %param.27) | copy-start | bytes 8650756
  6.5 1.8 copy-start.1
  6.5 215.3 %all-reduce.4.cloned.1.call-start = ((), (), s32[]{:S(2)}) async-start(), calls=%async_computation | async-start | bytes 262144 | tf_op jit(solution)/shard_map/psum | solution.py:80
  8.3 90.7 %copy-start.2 = (bf16[4,16,1024]{2,1,0:T(8,128)(2,1)S(1)}, bf16[4,16,1024]{2,1,0:T(8,128)(2,1)}, u32[]{:S(2)}) copy-start(bf16[4,16,1024]{2,1,0:T(8,128)(2,1)} %param.14) | copy-start | bytes 393220
  8.3 90.8 %copy-start.10 = (f32[1024]{0:T(1024)S(1)}, f32[1024]{0:T(1024)}, u32[]{:S(2)}) copy-start(f32[1024]{0:T(1024)} %param.20) | copy-start | bytes 12292
  101.7 4.7 %copy-start.6 = (bf16[4,16,4,64]{3,2,1,0:T(4,128)(2,1)}, bf16[4,16,4,64]{3,2,1,0:T(4,128)(2,1)S(1)}, u32[]{:S(2)}) copy-start(bf16[4,16,4,64]{3,2,1,0:T(4,128)(2,1)S(1)} %reshape_squeeze.9) | copy-start | bytes 98308
  101.7 4.0 copy-start.13
  147.4 4.2 %copy-start.5 = (f32[4,16,4]{0,2,1:T(4,128)}, f32[4,16,4]{0,2,1:T(4,128)S(1)}, u32[]{:S(2)}) copy-start(f32[4,16,4]{0,2,1:T(4,128)S(1)} %pmax.7) | copy-start | bytes 3076
  154.7 103.9 %all-reduce.6.cloned.1.call-start = ((), (), s32[]{:S(2)}) async-start(), calls=%async_computation.1 | async-start | bytes 524288 | tf_op jit(solution)/shard_map/psum | solution.py:123
  190.4 35.0 %copy-start.4 = (bf16[256,1024]{1,0:T(8,128)(2,1)S(1)}, bf16[256,1024]{1,0:T(8,128)(2,1)}, u32[]{:S(2)}) copy-start(bf16[256,1024]{1,0:T(8,128)(2,1)} %param.23) | copy-start | bytes 1572868
  191.6 0.7 copy-start.7
  191.6 0.8 copy-start.8
  221.9 37.8 %copy-start.12 = (f32[1024]{0:T(1024)S(1)}, f32[1024]{0:T(1024)}, u32[]{:S(2)}) copy-start(f32[1024]{0:T(1024)} %param.21) | copy-start | bytes 12292
  227.1 165.4 %all-reduce.8.cloned.1.call-start = ((), (), s32[]{:S(2)}) async-start(), calls=%async_computation.2 | async-start | bytes 524288 | tf_op jit(solution)/shard_map/psum | solution.py:141
  260.7 4.5 %copy-start.9 = (bf16[1024,16]{0,1:T(8,128)(2,1)S(1)}, bf16[1024,16]{0,1:T(8,128)(2,1)}, u32[]{:S(2)}) copy-start(bf16[1024,16]{0,1:T(8,128)(2,1)} %param.24) | copy-start | bytes 98308
  260.7 4.7 %copy-start.11 = (s32[4,16,2]{1,2,0:T(2,128)S(1)}, s32[4,16,2]{1,2,0:T(2,128)}, u32[]{:S(2)}) copy-start(s32[4,16,2]{1,2,0:T(2,128)} %param.25) | copy-start | bytes 1540
  266.1 126.5 %copy-start.3 = (f32[4,16,1024]{2,1,0:T(8,128)S(1)}, f32[4,16,1024]{2,1,0:T(8,128)}, u32[]{:S(2)}) copy-start(f32[4,16,1024]{2,1,0:T(8,128)} %all-reduce.6.cloned.1.call-done) | copy-start | bytes 786436
Sparse Core Ops, SparseCore 0:
  154.8 67.0 all-reduce.3
  227.3 31.2 all-reduce.5
  267.6 124.9 all-reduce.7
where the time goes:
time: 402 us; the launch traced here: 401 us
  waiting for transfers between devices  183 us (46%)
  local copies, waits for them, and re-layouts  105 us (26%)
  blocking collectives  72.5 us (18%)
  matrix products  18.5 us (5%)
  between operations  13.4 us (3%)
  other arithmetic  7.9 us (2%)
    psum x1, waiting for transfers between devices, layer(): mixture = lax.psum(expert_part, ('seq', 'tp'))  125 us
    gather x2, local copies, waits for them, and re-layouts, cache_part(): buckets = jnp.take(bucket_table, jnp.clip(distance, 0, table_len - 1))  90.6 us
    pmax x1, blocking collectives, merge_cache(): overall = lax.pmax(maxima, 'seq')  38.8 us
    psum x1, blocking collectives, merge_cache(): lax.psum((totals * factor, summed * factor[..., None]), 'seq')  33.7 us
    psum x1, waiting for transfers between devices, layer(): lax.psum(partial_value, 'tp')  31.3 us
    psum x1, waiting for transfers between devices, merge_cache(): lax.psum((totals * factor, summed * factor[..., None]), 'seq')  26.5 us
    unnamed x31, local copies, waits for them, and re-layouts  8.62 us
  transfers between devices with their start and end apart: 3, of which 3 were waited for; matrix products, arithmetic and copies ran while one was open for 2% of the time, Pallas kernels for 0%

commit v1 on v0

--- a/solution.py
+++ b/solution.py
@@ -138,7 +138,7 @@
             jnp.bfloat16
         )
         expert_part = jnp.einsum("srf,fd->srd", hidden, w_down, preferred_element_type=jnp.float32)
-        mixture = lax.psum(expert_part, ("seq", "tp"))
+        mixture = lax.psum(lax.psum(expert_part, "tp"), "seq")
         return (mid + mixture).astype(jnp.bfloat16)
 
     return layer(0, steps_all)

time: 402 us -> 383 us (0.953)
  waiting for transfers between devices: 183 us -> 164 us
    psum x1 -> x2, waiting for transfers between devices: 125 us -> 106 us  [layer(): mixture = lax.psum(lax.psum(expert_part, 'tp'), 'seq')]
  transfers between devices with their start and end apart: 3 -> 4, of which waited for: 3 -> 4; matrix products, arithmetic and copies ran while one was open for 2% -> 2% of each run, Pallas kernels for 0% -> 0%
where the time goes in v1:
time: 383 us; the launch traced here: 382 us
  waiting for transfers between devices  164 us (43%)
  local copies, waits for them, and re-layouts  105 us (27%)
  blocking collectives  72.5 us (19%)
  matrix products  18.5 us (5%)
  between operations  13.5 us (4%)
  other arithmetic  7.9 us (2%)
    psum x2, waiting for transfers between devices, layer(): mixture = lax.psum(lax.psum(expert_part, 'tp'), 'seq')  106 us
    gather x2, local copies, waits for them, and re-layouts, cache_part(): buckets = jnp.take(bucket_table, jnp.clip(distance, 0, table_len - 1))  90.6 us
    pmax x1, blocking collectives, merge_cache(): overall = lax.pmax(maxima, 'seq')  38.8 us
    psum x1, blocking collectives, merge_cache(): lax.psum((totals * factor, summed * factor[..., None]), 'seq')  33.7 us
    psum x1, waiting for transfers between devices, layer(): lax.psum(partial_value, 'tp')  31.3 us
    psum x1, waiting for transfers between devices, merge_cache(): lax.psum((totals * factor, summed * factor[..., None]), 'seq')  26.5 us
    unnamed x31, local copies, waits for them, and re-layouts  8.62 us
  transfers between devices with their start and end apart: 4, of which 4 were waited for; matrix products, arithmetic and copies ran while one was open for 2% of the time, Pallas kernels for 0%

profile of v1, /device:TPU:0, one launch (start us, length us, event | category | flops | bytes accessed | tf_op | source)
XLA Modules:
  0.0 381.9 jit_solution(2140841947518368692)
XLA Ops:
  6.5 0.8 iota_add_fusion.1
  7.4 0.8 broadcast_compare_fusion
  8.2 0.1 compare_select_fusion
  8.3 90.5 %gather_fusion = s32[16384]{0:T(1024)S(1)} fusion(s32[2052]{0:T(1024)S(1)} %copy-done.1, s32[16384]{0:T(1024)S(1)} %broadcast_clamp_fusion), kind=kCustom, calls=%fused_computation | custom fusion | bytes 196608 | tf_op jit(solution)/shard_map/jit(_take)/gather | solution.py:63
  98.9 0.1 fusion.59
  99.0 0.1 fusion.37
  99.2 1.8 fusion.23
  101.0 0.6 fusion.78
  101.6 0.1 reshape_squeeze.9
  101.7 4.0 %copy.81 = bf16[16,256,256]{1,2,0:T(8,128)(2,1)} copy(bf16[16,256,256]{2,1,0:T(8,128)(2,1)} %param.15) | data formatting | bytes 4194304 | tf_op args[1]
  105.7 0.7 fusion.8
  106.4 2.1 fusion.80
  108.6 38.8 %pmax.7 = f32[4,16,4]{0,2,1:T(4,128)S(1)} all-reduce(f32[4,16,4]{0,2,1:T(4,128)S(1)} %get-tuple-element.17), channel_id=1, replica_groups=mesh['seq'=8,'tp'=4] {'seq'}, use_global_device_ids=true, to_apply=%region_2.3 | all-reduce | flops 256 | bytes 2048 | tf_op jit(solution)/shard_map/pmax | solution.py:78
  147.4 0.3 fusion.40
  147.7 3.9 %copy.84 = bf16[16,256,256]{1,2,0:T(8,128)(2,1)} copy(bf16[16,256,256]{2,1,0:T(8,128)(2,1)} %param.16) | data formatting | bytes 4194304 | tf_op args[2]
  151.7 3.0 fusion.16
  154.7 0.0 all-reduce.7.cloned.1.call-start
  154.7 33.7 %psum.36 = f32[4,16,4]{0,2,1:T(4,128)} all-reduce(f32[4,16,4]{0,2,1:T(4,128)S(1)} %bitcast.133), channel_id=1, replica_groups=mesh['seq'=8,'tp'=4] {'seq'}, use_global_device_ids=true, to_apply=%region_6.7 | all-reduce | flops 256 | bytes 2048 | tf_op jit(solution)/shard_map/psum | solution.py:80
  188.4 0.7 reshape_squeeze.10
  189.1 0.1 copy.85
  189.2 0.1 reshape.206
  189.3 0.7 gather_fusion.1
  190.0 0.1 reshape.205
  190.1 0.2 convolution_bitcast_fusion.4
  190.3 0.1 copy.88
  190.4 1.2 fusion.81
  191.6 0.6 copy-done.7
  192.3 0.1 fusion.51
  192.4 1.4 multiply_add_fusion
  193.9 1.5 reshape_squeeze.11
  195.3 26.5 %all-reduce.5.cloned.1.call-done = f32[4,16,4,64]{3,0,2,1:T(4,128)} async-done(((f32[4,16,4,64]{3,0,2,1:T(4,128)}), f32[4,16,4,64]{3,0,2,1:T(4,128)}) %all-reduce.5.cloned.1.call-update) | async-done | bytes 65552 | tf_op jit(solution)/shard_map/psum | solution.py:80
  221.9 1.4 fusion.22
  223.2 0.7 copy.91
  223.9 1.6 convert_element_type.36
  225.5 1.7 fusion.27
  227.1 0.0 all-reduce.9.cloned.1.call-start
  227.2 31.3 %all-reduce.7.cloned.1.call-done = f32[4,16,1024]{2,1,0:T(8,128)} async-done(((f32[4,16,1024]{2,1,0:T(8,128)}), f32[4,16,1024]{2,1,0:T(8,128)}) %all-reduce.7.cloned.1.call-update) | async-done | bytes 262160 | tf_op jit(solution)/shard_map/psum | solution.py:123
  258.5 1.1 multiply_reduce_fusion
  259.6 1.1 multiply_convert_fusion
  260.7 4.5 %fusion.4 = f32[2,4,16,1408]{3,2,0,1:T(8,128)S(1)} fusion(bf16[2,1408,1024]{2,1,0:T(8,128)(2,1)} %param.26, bf16[4,16,1024]{2,1,0:T(8,128)(2,1)S(1)} %multiply_convert_fusion), kind=kOutput, calls=%fused_computation.6 | convolution fusion | flops 369098752 | bytes 6619136 | tf_op jit(solution)/shard_map/srd,kfd->ksrf/dot_general | solution.py:136
  265.2 0.2 fusion.66
  265.4 0.2 select_reduce_fusion.1
  265.6 0.1 select_reduce_fusion
  265.7 0.3 fusion.7
  266.1 1.3 fusion.2
  267.5 32.1 %all-reduce.9.cloned.1.call-done = f32[4,16,1024]{2,1,0:T(8,128)} async-done(((f32[4,16,1024]{2,1,0:T(8,128)}), f32[4,16,1024]{2,1,0:T(8,128)}) %all-reduce.9.cloned.1.call-update) | async-done | bytes 262160 | tf_op jit(solution)/shard_map/psum | solution.py:141
  299.6 74.1 %all-reduce.11.cloned.1.call-done = f32[4,16,1024]{2,1,0:T(8,128)} async-done(((f32[4,16,1024]{2,1,0:T(8,128)}), f32[4,16,1024]{2,1,0:T(8,128)}) %all-reduce.11.cloned.1.call-update) | async-done | bytes 262160 | tf_op jit(solution)/shard_map/psum | solution.py:141
  373.7 1.6 add_convert_fusion
  (49 shorter events, 0.3 us)
Async XLA Ops:
  6.5 259.5 %copy-start = (bf16[1408,1024]{1,0:T(8,128)(2,1)S(1)}, bf16[1408,1024]{1,0:T(8,128)(2,1)}, u32[]{:S(2)}) copy-start(bf16[1408,1024]{1,0:T(8,128)(2,1)} %param.27) | copy-start | bytes 8650756
  6.5 1.8 copy-start.1
  6.5 215.3 %all-reduce.5.cloned.1.call-start = ((), (), s32[]{:S(2)}) async-start(), calls=%async_computation | async-start | bytes 262144 | tf_op jit(solution)/shard_map/psum | solution.py:80
  8.3 90.7 %copy-start.2 = (bf16[4,16,1024]{2,1,0:T(8,128)(2,1)S(1)}, bf16[4,16,1024]{2,1,0:T(8,128)(2,1)}, u32[]{:S(2)}) copy-start(bf16[4,16,1024]{2,1,0:T(8,128)(2,1)} %param.14) | copy-start | bytes 393220
  8.3 90.8 %copy-start.10 = (f32[1024]{0:T(1024)S(1)}, f32[1024]{0:T(1024)}, u32[]{:S(2)}) copy-start(f32[1024]{0:T(1024)} %param.20) | copy-start | bytes 12292
  101.7 4.7 %copy-start.6 = (bf16[4,16,4,64]{3,2,1,0:T(4,128)(2,1)}, bf16[4,16,4,64]{3,2,1,0:T(4,128)(2,1)S(1)}, u32[]{:S(2)}) copy-start(bf16[4,16,4,64]{3,2,1,0:T(4,128)(2,1)S(1)} %reshape_squeeze.9) | copy-start | bytes 98308
  101.7 4.0 %copy-start.13 = (f32[32,4]{0,1:T(4,128)S(1)}, f32[32,4]{0,1:T(4,128)}, u32[]{:S(2)}) copy-start(f32[32,4]{0,1:T(4,128)} %param.19) | copy-start | bytes 1540
  147.4 4.2 %copy-start.5 = (f32[4,16,4]{0,2,1:T(4,128)}, f32[4,16,4]{0,2,1:T(4,128)S(1)}, u32[]{:S(2)}) copy-start(f32[4,16,4]{0,2,1:T(4,128)S(1)} %pmax.7) | copy-start | bytes 3076
  154.7 103.9 %all-reduce.7.cloned.1.call-start = ((), (), s32[]{:S(2)}) async-start(), calls=%async_computation.1 | async-start | bytes 524288 | tf_op jit(solution)/shard_map/psum | solution.py:123
  190.4 35.0 %copy-start.4 = (bf16[256,1024]{1,0:T(8,128)(2,1)S(1)}, bf16[256,1024]{1,0:T(8,128)(2,1)}, u32[]{:S(2)}) copy-start(bf16[256,1024]{1,0:T(8,128)(2,1)} %param.23) | copy-start | bytes 1572868
  191.6 0.7 copy-start.7
  191.6 0.8 copy-start.8
  221.9 37.8 %copy-start.12 = (f32[1024]{0:T(1024)S(1)}, f32[1024]{0:T(1024)}, u32[]{:S(2)}) copy-start(f32[1024]{0:T(1024)} %param.21) | copy-start | bytes 12292
  227.1 72.4 %all-reduce.9.cloned.1.call-start = ((), (), s32[]{:S(2)}) async-start(), calls=%async_computation.2 | async-start | bytes 524288 | tf_op jit(solution)/shard_map/psum | solution.py:141
  260.7 4.5 %copy-start.9 = (bf16[1024,16]{0,1:T(8,128)(2,1)S(1)}, bf16[1024,16]{0,1:T(8,128)(2,1)}, u32[]{:S(2)}) copy-start(bf16[1024,16]{0,1:T(8,128)(2,1)} %param.24) | copy-start | bytes 98308
  260.7 4.7 %copy-start.11 = (s32[4,16,2]{1,2,0:T(2,128)S(1)}, s32[4,16,2]{1,2,0:T(2,128)}, u32[]{:S(2)}) copy-start(s32[4,16,2]{1,2,0:T(2,128)} %param.25) | copy-start | bytes 1540
  266.1 107.6 %copy-start.3 = (f32[4,16,1024]{2,1,0:T(8,128)S(1)}, f32[4,16,1024]{2,1,0:T(8,128)}, u32[]{:S(2)}) copy-start(f32[4,16,1024]{2,1,0:T(8,128)} %all-reduce.7.cloned.1.call-done) | copy-start | bytes 786436
  267.5 106.3 %all-reduce.11.cloned.1.call-start = ((), (), s32[]{:S(2)}) async-start(), calls=%async_computation.3 | async-start | bytes 524288 | tf_op jit(solution)/shard_map/psum | solution.py:141
Sparse Core Ops, SparseCore 0:
  154.8 67.0 all-reduce.4
  227.3 31.2 all-reduce.6
  267.6 31.9 all-reduce.8
  303.2 70.5 all-reduce.10
